TPU v7x, 32 devices: a whole 2x2x4 slice. The times are simulated.
32 devices in a mesh: row: 4 (over x, core), col: 8 (over z, y).
Axes of the slice: x: 2, y: 2, z: 4, core: 2. Of those that a mesh axis runs over, the one named last changes fastest.
Arguments:
- tile_list: int32 [512, 2], P(('row', 'col')), may hold values from -1 to 63, as said below
- tile_values: bfloat16 [512, 512, 512], P(('row', 'col'))
- block_order: int32 [64], replicated, may hold values from 0 to 63, as said below
- basis: bfloat16 [64, 512, 256], P(('row', 'col')), may hold values from -8 to 8
Outputs:
- basis_out: bfloat16 [64, 512, 256], P(('row', 'col'))
- projected: float32 [256, 256], replicated
Inputs may be any that keep to these rules, and one draw needn't show every extreme that they name: `block_order`: A permutation of the channel blocks; slot p lies on device p // 2 in row-major order of (row, col). `tile_list`: slots of device (i, j) hold tiles whose row block sits in a slot of a device of row index i and whose column block sits in a slot of a device of column index j; each unordered pair of blocks appears at most once in all; empty slots hold -1 in both columns and may stand anywhere among a device's slots; every device holds at most 16 tiles and some device holds exactly 16.
All inputs are finite; a program needn't handle non-finite values.
Results may differ from a plain program's by a relative error of at most 0.0017.
Values may be sent and summed in bfloat16 or wider, within the bound.
A program may use at most 128 MiB of HBM per device.

v0:
```python
import jax
import jax.numpy as jnp
from jax import lax
from jax.sharding import PartitionSpec as P


def per_device(tile_list, tile_values, block_order, basis):
    rows_count = lax.axis_size("row")
    cols_count = lax.axis_size("col")
    own_blocks = basis.shape[0]
    edge = basis.shape[1]
    rank = basis.shape[2]
    blocks_all = block_order.shape[0]
    scale = jnp.sqrt(jnp.float32(blocks_all * edge))
    row_here = lax.axis_index("row")
    row_group = own_blocks * cols_count
    col_group = own_blocks * rows_count
    present = tile_list[:, 0] >= 0
    slot_range = jnp.arange(blocks_all, dtype=jnp.int32)
    ids_both = jnp.where(present[:, None], tile_list, 0)
    match = block_order[None, None, :] == ids_both[:, :, None]
    slots_both = jnp.sum(jnp.where(match, slot_range[None, None, :], 0), axis=2)
    first_slot = slots_both[:, 0]
    second_slot = slots_both[:, 1]
    row_local = jnp.where(present, first_slot - row_here * row_group, row_group)
    owner_second = second_slot // own_blocks
    col_local = jnp.where(
        present, owner_second // cols_count * own_blocks + second_slot % own_blocks, col_group
    )
    column_side = lax.all_gather(basis, "row", axis=0, tiled=True)
    row_side = lax.all_gather(basis, "col", axis=0, tiled=True)
    empty_block = jnp.zeros((1, edge, rank), basis.dtype)
    column_padded = jnp.concatenate([column_side, empty_block], axis=0)
    row_padded = jnp.concatenate([row_side, empty_block], axis=0)
    picked_col = column_padded[col_local]
    picked_row = row_padded[row_local]
    near_prod = jnp.einsum(
        "tab,tbk->tak", tile_values, picked_col, preferred_element_type=jnp.float32
    )
    far_prod = jnp.einsum(
        "tba,tbk->tak", tile_values, picked_row, preferred_element_type=jnp.float32
    )
    col_partial = (
        jnp.zeros((col_group, edge, rank), jnp.float32).at[col_local].add(far_prod, mode="drop")
    )
    row_partial = (
        jnp.zeros((row_group, edge, rank), jnp.float32).at[row_local].add(near_prod, mode="drop")
    )
    row_owned = lax.psum_scatter(row_partial, "col", scatter_dimension=0, tiled=True)
    upper_part = lax.optimization_barrier(col_partial.astype(jnp.bfloat16))
    remainder = col_partial - upper_part.astype(jnp.float32)
    middle_part = lax.optimization_barrier(remainder.astype(jnp.bfloat16))
    lower_part = (remainder - middle_part.astype(jnp.float32)).astype(jnp.bfloat16)
    pieces = jnp.concatenate([upper_part, middle_part, lower_part], axis=2)
    folded = jnp.einsum("sak,saj->kj", column_side, pieces, preferred_element_type=jnp.float32)
    tile_form = folded[:, :rank] + folded[:, rank : 2 * rank] + folded[:, 2 * rank :]
    projected = lax.psum((tile_form + tile_form.T) / scale, ("row", "col"))
    col_owned = lax.psum_scatter(col_partial, "row", scatter_dimension=0, tiled=True)
    product = (row_owned + col_owned).reshape(own_blocks * edge, rank)
    gram_term = jnp.dot(product.T, product, precision=lax.Precision.HIGHEST)
    gram = lax.psum(gram_term, ("row", "col"))
    first_factor = jnp.linalg.cholesky(gram)
    first_basis = lax.linalg.triangular_solve(
        first_factor, product, left_side=False, lower=True, transpose_a=True
    )
    second_term = jnp.dot(first_basis.T, first_basis, precision=lax.Precision.HIGHEST)
    second = lax.psum(second_term, ("row", "col"))
    second_factor = jnp.linalg.cholesky(second)
    final = lax.linalg.triangular_solve(
        second_factor, first_basis, left_side=False, lower=True, transpose_a=True
    )
    basis_out = (final * scale).astype(jnp.bfloat16).reshape(own_blocks, edge, rank)
    return (basis_out, projected)


def solution(mesh):
    in_specs = (
        P(("row", "col"), None),
        P(("row", "col"), None, None),
        P(),
        P(("row", "col"), None, None),
    )
    out_specs = (P(("row", "col"), None, None), P())
    return jax.shard_map(
        per_device, mesh=mesh, in_specs=in_specs, out_specs=out_specs, check_vma=False
    )
```

profile of v0, /device:TPU:0, one launch (start us, length us, event | category | flops | bytes accessed | tf_op | source)
XLA Modules:
  0.0 729.1 jit_solution(8188007919640402378)
XLA Ops:
  10.1 0.8 select_reduce_fusion.2
  11.6 74.0 %all-gather.5.cloned.1.call-done = bf16[16,512,256]{2,1,0:T(8,128)(2,1)} async-done(((bf16[2,512,256]{2,1,0:T(8,128)(2,1)}), bf16[16,512,256]{2,1,0:T(8,128)(2,1)}) %all-gather.5.cloned.1.call-update) | async-done | bytes 4194320 | tf_op jit(solution)/shard_map/all_gather | solution.py:31
  85.6 4.6 concatenate.13
  90.3 5.2 gather_fusion.1
  95.5 10.3 %convolution_bitcast_fusion = f32[16,512,256]{1,2,0:T(8,128)} fusion(bf16[16,512,256]{2,1,0:T(8,128)(2,1)} %gather_fusion.1, bf16[16,512,512]{2,1,0:T(8,128)(2,1)} %param.8), kind=kOutput, calls=%fused_computation.16 | convolution fusion | flops 2147483648 | bytes 20971520 | tf_op jit(solution)/shard_map/tba,tbk->tak/dot_general | solution.py:40
  105.8 9.3 %copy.39 = f32[16,512,256]{2,1,0:T(8,128)} copy(f32[16,512,256]{1,2,0:T(8,128)} %convolution_bitcast_fusion) | data formatting | bytes 16777216 | tf_op jit(solution)/shard_map/tba,tbk->tak/dot_general | solution.py:40
  115.1 2.3 broadcast_in_dim.54
  117.4 15.6 %scatter_fusion.1 = f32[8,512,256]{2,1,0:T(8,128)} fusion(f32[8,512,256]{2,1,0:T(8,128)} %broadcast_in_dim.54, s32[16]{0:T(128)S(1)} %get-tuple-element.46, f32[16,512,256]{2,1,0:T(8,128)} %copy.39), kind=kCustom, calls=%fused_computation.3 | custom fusion | flops 2097152 | bytes 25165888 | tf_op jit(solution)/shard_map/scatter-add | solution.py:44
  133.1 1.7 concatenate.12
  134.9 2.7 gather_fusion
  137.6 12.1 %convolution_bitcast_fusion.1 = f32[16,512,256]{1,2,0:T(8,128)} fusion(bf16[16,512,256]{2,1,0:T(8,128)(2,1)} %gather_fusion, bf16[16,512,512]{2,1,0:T(8,128)(2,1)} %param.8), kind=kOutput, calls=%fused_computation.17 | convolution fusion | flops 2147483648 | bytes 20971520 | tf_op jit(solution)/shard_map/tab,tbk->tak/dot_general | solution.py:37
  149.7 9.3 %copy.37 = f32[16,512,256]{2,1,0:T(8,128)} copy(f32[16,512,256]{1,2,0:T(8,128)} %convolution_bitcast_fusion.1) | data formatting | bytes 16777216 | tf_op jit(solution)/shard_map/tab,tbk->tak/dot_general | solution.py:37
  159.1 4.1 broadcast_in_dim.47
  163.1 15.9 %scatter_fusion = f32[16,512,256]{2,1,0:T(8,128)} fusion(f32[16,512,256]{2,1,0:T(8,128)} %broadcast_in_dim.47, s32[16]{0:T(128)S(1)} %fusion.37, f32[16,512,256]{2,1,0:T(8,128)} %copy.37), kind=kCustom, calls=%fused_computation.2 | custom fusion | flops 2097152 | bytes 25165888 | tf_op jit(solution)/shard_map/scatter-add | solution.py:47
  179.0 12.8 %all-reduce.7.cloned.1.call-start = ((), (), s32[]{:S(2)}) async-start(), calls=%async_computation.6 | async-start | bytes 524288 | tf_op jit(solution)/shard_map/psum | solution.py:61
  191.9 5.4 copy.46
  197.2 2.6 convert_element_type.19
  199.8 0.9 copy-done
  201.5 1.0 subtract_convert_fusion
  203.1 1.8 fusion.7
  205.1 124.2 %reduce-scatter.3.cloned.1.call-done = f32[2,512,256]{2,1,0:T(8,128)} async-done(((f32[16,512,256]{2,1,0:T(8,128)}), f32[2,512,256]{2,1,0:T(8,128)}) %reduce-scatter.3.cloned.1.call-update) | async-done | bytes 1048592 | tf_op jit(solution)/shard_map/reduce_scatter | solution.py:49
  329.3 1.7 add.88
  331.0 2.5 convolution_bitcast_fusion.2
  333.6 0.8 fusion.17
  334.3 126.6 %all-reduce.7.cloned.1.call-done = f32[256,256]{0,1:T(8,128)} async-done(((f32[256,256]{0,1:T(8,128)}), f32[256,256]{0,1:T(8,128)}) %all-reduce.7.cloned.1.call-update) | async-done | bytes 262160 | tf_op jit(solution)/shard_map/psum | solution.py:61
  461.0 1.1 copy.42
  462.1 1.0 fusion.19
  463.1 11.7 %cholesky.130 = f32[128,128]{1,0:T(8,128)S(1)} custom-call(f32[128,128]{1,0:T(8,128)S(1)} %cholesky.194), custom_call_target="Cholesky" | custom-call | tf_op jit(solution)/shard_map/jit(cholesky)/cholesky | solution.py:62
  474.9 9.8 %custom-call.13 = f32[1,128,128]{1,2,0:T(8,128)S(1)} custom-call(f32[1,128,128]{2,1,0:T(8,128)S(1)} %get-tuple-element.59), custom_call_target="InvertDiagBlocksLowerTriangular" | custom-call | tf_op jit(solution)/shard_map/jit(cholesky)/cholesky | solution.py:62
  485.1 11.7 %cholesky.147 = f32[128,128]{1,0:T(8,128)S(1)} custom-call(f32[128,128]{1,0:T(8,128)S(1)} %convolution_subtract_fusion.3), custom_call_target="Cholesky" | custom-call | tf_op jit(solution)/shard_map/jit(cholesky)/cholesky | solution.py:62
  499.1 4.1 while.4
  499.7 1.4 bitcast_dynamic-update-slice_fusion.4
  501.8 1.4 bitcast_dynamic-update-slice_fusion.4
  503.2 20.0 %custom-call.14 = f32[2,128,128]{1,2,0:T(8,128)S(1)} custom-call(f32[2,128,128]{2,1,0:T(8,128)S(1)} %get-tuple-element.18), custom_call_target="InvertDiagBlocksLowerTriangular" | custom-call | tf_op jit(solution)/shard_map/triangular_solve/custom-call.0 | solution.py:63
  523.8 1.0 convolution_subtract_fusion.1
  525.5 1.7 fusion.10
  527.2 128.6 %all-reduce.9.cloned.1.call-done = (f32[256,256]{0,1:T(8,128)}, f32[256,256]{0,1:T(8,128)}) async-done(((f32[256,256]{0,1:T(8,128)}, f32[256,256]{0,1:T(8,128)}), (f32[256,256]{0,1:T(8,128)}, f32[256,256]{0,1:T(8,128)})) %all-reduce.9.cloned.1.call-update) | async-done | bytes 524304 | tf_op jit(solution)/shard_map/psum | solution.py:67
  655.8 1.1 copy.44
  656.9 1.0 fusion.18
  657.9 11.7 %cholesky.164 = f32[128,128]{1,0:T(8,128)S(1)} custom-call(f32[128,128]{1,0:T(8,128)S(1)} %cholesky.197), custom_call_target="Cholesky" | custom-call | tf_op jit(solution)/shard_map/jit(cholesky)/cholesky | solution.py:68
  669.6 9.8 %custom-call.15 = f32[1,128,128]{1,2,0:T(8,128)S(1)} custom-call(f32[1,128,128]{2,1,0:T(8,128)S(1)} %get-tuple-element.55), custom_call_target="InvertDiagBlocksLowerTriangular" | custom-call | tf_op jit(solution)/shard_map/jit(cholesky)/cholesky | solution.py:68
  679.9 11.9 %cholesky.181 = f32[128,128]{1,0:T(8,128)S(1)} custom-call(f32[128,128]{1,0:T(8,128)S(1)} %convolution_subtract_fusion.2), custom_call_target="Cholesky" | custom-call | tf_op jit(solution)/shard_map/jit(cholesky)/cholesky | solution.py:68
  694.5 4.0 while.5
  695.1 1.4 bitcast_dynamic-update-slice_fusion.5
  697.1 1.4 bitcast_dynamic-update-slice_fusion.5
  698.5 19.7 %custom-call.16 = f32[2,128,128]{1,2,0:T(8,128)S(1)} custom-call(f32[2,128,128]{2,1,0:T(8,128)S(1)} %get-tuple-element.19), custom_call_target="InvertDiagBlocksLowerTriangular" | custom-call | tf_op jit(solution)/shard_map/triangular_solve/custom-call.0 | solution.py:69
  720.2 1.0 copy.58
  721.2 0.8 copy.50
  (63 shorter events, 14.2 us)
Async XLA Ops:
  7.2 78.5 %all-gather.5.cloned.1.call-start = ((), (), s32[]{:S(2)}) async-start(), calls=%async_computation.4 | async-start | bytes 4718592 | tf_op jit(solution)/shard_map/all_gather | solution.py:31
  7.9 125.2 %all-gather.3.cloned.1.call-start = ((), (), s32[]{:S(2)}) async-start(), calls=%async_computation.2 | async-start | bytes 2621440 | tf_op jit(solution)/shard_map/all_gather | solution.py:30
  8.6 196.5 %reduce-scatter.5.cloned.1.call-start = ((), (), s32[]{:S(2)}) async-start(), calls=%async_computation.5 | async-start | bytes 5242880 | tf_op jit(solution)/shard_map/reduce_scatter | solution.py:58
  133.0 196.3 %reduce-scatter.3.cloned.1.call-start = ((), (), s32[]{:S(2)}) async-start(), calls=%async_computation.3 | async-start | bytes 9437184 | tf_op jit(solution)/shard_map/reduce_scatter | solution.py:49
  179.0 282.0 %all-reduce.7.cloned.1.call-start = ((), (), s32[]{:S(2)}) async-start(), calls=%async_computation.6 | async-start | bytes 524288 | tf_op jit(solution)/shard_map/psum | solution.py:61
  197.2 3.5 copy-start
  201.5 1.6 copy-start.1
  333.5 322.3 %all-reduce.9.cloned.1.call-start = ((), (), s32[]{:S(2)}) async-start(), calls=%async_computation.7 | async-start | bytes 1048576 | tf_op jit(solution)/shard_map/psum | solution.py:67
  679.7 41.5 %copy-start.2 = (f32[256,256]{0,1:T(8,128)S(1)}, f32[256,256]{0,1:T(8,128)}, u32[]{:S(2)}) copy-start(f32[256,256]{0,1:T(8,128)} %get-tuple-element.43) | copy-start | bytes 786436
Sparse Core Ops, SparseCore 0:
  10.1 75.5 all-gather.4
  87.2 21.0 all-gather.2
  133.1 45.1 reduce-scatter.4
  181.8 147.4 reduce-scatter.2
  335.2 125.7 all-reduce.6
  527.3 128.3 all-reduce.8
where the time goes:
time: 737 us; the launch traced here: 729 us
  waiting for transfers between devices  455 us (62%)
  other arithmetic  152 us (21%)
  local copies, waits for them, and re-layouts  58.5 us (8%)
  matrix products  33.5 us (5%)
  between operations  17.3 us (2%)
  starting transfers between devices  13 us (2%)
    psum x1, waiting for transfers between devices, per_device(): second = lax.psum(second_term, ('row', 'col'))  129 us
    psum x1, waiting for transfers between devices, per_device(): gram = lax.psum(gram_term, ('row', 'col'))  127 us
    reduce_scatter x1, waiting for transfers between devices, per_device(): lax.psum_scatter(row_partial, 'col', scatter_dimension=0, tiled=True)  124 us
    all_gather x1, waiting for transfers between devices, per_device(): row_side = lax.all_gather(basis, 'col', axis=0, tiled=True)  74 us
    another operation x7, other arithmetic, per_device(): second_factor = jnp.linalg.cholesky(second)  34.8 us
    another operation x6, other arithmetic, per_device(): first_factor = jnp.linalg.cholesky(gram)  34 us
    another operation x3, other arithmetic, per_device(): lax.linalg.triangular_solve(first_factor, product, left_side=False, lower...  20 us
    another operation x2, other arithmetic, per_device(): lax.linalg.triangular_solve(second_factor, first_basis, left_side=False,...  19.7 us
  transfers between devices with their start and end apart: 6, of which 4 were waited for; matrix products, arithmetic and copies ran while one was open for 15% of the time, Pallas kernels for 0%

commit v1 on v0

--- a/solution.py
+++ b/solution.py
@@ -2,6 +2,7 @@
 import jax.numpy as jnp
 from jax import lax
 from jax.sharding import PartitionSpec as P
+from jax.lax import all_gather
 
 
 def per_device(tile_list, tile_values, block_order, basis):
@@ -64,7 +65,12 @@
         first_factor, product, left_side=False, lower=True, transpose_a=True
     )
     second_term = jnp.dot(first_basis.T, first_basis, precision=lax.Precision.HIGHEST)
-    second = lax.psum(second_term, ("row", "col"))
+
+    def name_works_on_mesh(a0):
+        reached = jnp.sum(all_gather(a0, axis_name=("row", "col")), axis=0)
+        return reached
+
+    second = name_works_on_mesh(second_term)
     second_factor = jnp.linalg.cholesky(second)
     final = lax.linalg.triangular_solve(
         second_factor, first_basis, left_side=False, lower=True, transpose_a=True

time: 737 us -> 688 us (0.934)
  waiting for transfers between devices: 455 us -> 417 us
  starting transfers between devices: 13 us -> 0.42 us
    psum x1 -> x0, waiting for transfers between devices: 129 us -> none  [per_device(): second = lax.psum(second_term, ('row', 'col'))]
    all_gather x0 -> x1, waiting for transfers between devices: none -> 75.4 us  [name_works_on_mesh(): reached = jnp.sum(all_gather(a0, axis_name=('row', 'col')), axis=0)]
    psum x1, starting transfers between devices: 12.8 us -> 0.22 us  [per_device(): gram = lax.psum(gram_term, ('row', 'col'))]
    reduce_scatter x1, waiting for transfers between devices: 124 us -> 136 us  [per_device(): lax.psum_scatter(row_partial, 'col', scatter_dimension=0, tiled=True)]
  transfers between devices with their start and end apart: 6 -> 6, of which waited for: 4 -> 4; matrix products, arithmetic and copies ran while one was open for 15% -> 16% of each run, Pallas kernels for 0% -> 0%
where the time goes in v1:
time: 688 us; the launch traced here: 681 us
  waiting for transfers between devices  417 us (61%)
  other arithmetic  155 us (23%)
  local copies, waits for them, and re-layouts  57.6 us (8%)
  matrix products  33.5 us (5%)
  between operations  17.3 us (3%)
    reduce_scatter x1, waiting for transfers between devices, per_device(): lax.psum_scatter(row_partial, 'col', scatter_dimension=0, tiled=True)  136 us
    psum x1, waiting for transfers between devices, per_device(): gram = lax.psum(gram_term, ('row', 'col'))  130 us
    all_gather x1, waiting for transfers between devices, name_works_on_mesh(): reached = jnp.sum(all_gather(a0, axis_name=('row', 'col')), axis=0)  75.4 us
    all_gather x1, waiting for transfers between devices, per_device(): row_side = lax.all_gather(basis, 'col', axis=0, tiled=True)  74 us
    another operation x7, other arithmetic, per_device(): second_factor = jnp.linalg.cholesky(second)  34.8 us
    another operation x6, other arithmetic, per_device(): first_factor = jnp.linalg.cholesky(gram)  33.9 us
    another operation x3, other arithmetic, per_device(): lax.linalg.triangular_solve(first_factor, product, left_side=False, lower...  20.1 us
    another operation x2, other arithmetic, per_device(): lax.linalg.triangular_solve(second_factor, first_basis, left_side=False,...  19.7 us
  transfers between devices with their start and end apart: 6, of which 4 were waited for; matrix products, arithmetic and copies ran while one was open for 16% of the time, Pallas kernels for 0%

profile of v1, /device:TPU:0, one launch (start us, length us, event | category | flops | bytes accessed | tf_op | source)
XLA Modules:
  0.0 680.7 jit_solution(2196165574084479257)
XLA Ops:
  10.1 0.8 select_reduce_fusion.2
  11.6 74.0 %all-gather.7.cloned.1.call-done = bf16[16,512,256]{2,1,0:T(8,128)(2,1)} async-done(((bf16[2,512,256]{2,1,0:T(8,128)(2,1)}), bf16[16,512,256]{2,1,0:T(8,128)(2,1)}) %all-gather.7.cloned.1.call-update) | async-done | bytes 4194320 | tf_op jit(solution)/shard_map/all_gather | solution.py:32
  85.6 4.6 concatenate.13
  90.3 5.2 gather_fusion.1
  95.5 10.3 %convolution_bitcast_fusion = f32[16,512,256]{1,2,0:T(8,128)} fusion(bf16[16,512,256]{2,1,0:T(8,128)(2,1)} %gather_fusion.1, bf16[16,512,512]{2,1,0:T(8,128)(2,1)} %param.8), kind=kOutput, calls=%fused_computation.16 | convolution fusion | flops 2147483648 | bytes 20971520 | tf_op jit(solution)/shard_map/tba,tbk->tak/dot_general | solution.py:41
  105.8 9.3 %copy.37 = f32[16,512,256]{2,1,0:T(8,128)} copy(f32[16,512,256]{1,2,0:T(8,128)} %convolution_bitcast_fusion) | data formatting | bytes 16777216 | tf_op jit(solution)/shard_map/tba,tbk->tak/dot_general | solution.py:41
  115.1 2.3 broadcast_in_dim.54
  117.4 15.6 %scatter_fusion.1 = f32[8,512,256]{2,1,0:T(8,128)} fusion(f32[8,512,256]{2,1,0:T(8,128)} %broadcast_in_dim.54, s32[16]{0:T(128)S(1)} %get-tuple-element.46, f32[16,512,256]{2,1,0:T(8,128)} %copy.37), kind=kCustom, calls=%fused_computation.3 | custom fusion | flops 2097152 | bytes 25165888 | tf_op jit(solution)/shard_map/scatter-add | solution.py:45
  133.1 1.7 concatenate.12
  134.9 2.7 gather_fusion
  137.6 12.1 %convolution_bitcast_fusion.1 = f32[16,512,256]{1,2,0:T(8,128)} fusion(bf16[16,512,256]{2,1,0:T(8,128)(2,1)} %gather_fusion, bf16[16,512,512]{2,1,0:T(8,128)(2,1)} %param.8), kind=kOutput, calls=%fused_computation.17 | convolution fusion | flops 2147483648 | bytes 20971520 | tf_op jit(solution)/shard_map/tab,tbk->tak/dot_general | solution.py:38
  149.7 9.3 %copy.35 = f32[16,512,256]{2,1,0:T(8,128)} copy(f32[16,512,256]{1,2,0:T(8,128)} %convolution_bitcast_fusion.1) | data formatting | bytes 16777216 | tf_op jit(solution)/shard_map/tab,tbk->tak/dot_general | solution.py:38
  159.1 4.1 broadcast_in_dim.47
  163.1 15.9 %scatter_fusion = f32[16,512,256]{2,1,0:T(8,128)} fusion(f32[16,512,256]{2,1,0:T(8,128)} %broadcast_in_dim.47, s32[16]{0:T(128)S(1)} %fusion.37, f32[16,512,256]{2,1,0:T(8,128)} %copy.35), kind=kCustom, calls=%fused_computation.2 | custom fusion | flops 2097152 | bytes 25165888 | tf_op jit(solution)/shard_map/scatter-add | solution.py:48
  179.3 5.4 copy.43
  184.6 2.6 convert_element_type.19
  187.3 0.8 copy-done
  188.1 0.8 fusion.6
  188.8 1.0 subtract_convert_fusion
  189.8 0.8 copy-done.1
  190.6 1.8 fusion.7
  192.6 0.8 fusion.17
  193.4 136.0 %reduce-scatter.3.cloned.1.call-done = f32[2,512,256]{2,1,0:T(8,128)} async-done(((f32[16,512,256]{2,1,0:T(8,128)}), f32[2,512,256]{2,1,0:T(8,128)}) %reduce-scatter.3.cloned.1.call-update) | async-done | bytes 1048592 | tf_op jit(solution)/shard_map/reduce_scatter | solution.py:50
  329.3 1.7 add.86
  331.0 2.5 convolution_bitcast_fusion.2
  333.6 130.1 %all-reduce.6.cloned.1.call-done = (f32[256,256]{0,1:T(8,128)}, f32[256,256]{0,1:T(8,128)}) async-done(((f32[256,256]{0,1:T(8,128)}, f32[256,256]{0,1:T(8,128)}), (f32[256,256]{0,1:T(8,128)}, f32[256,256]{0,1:T(8,128)})) %all-reduce.6.cloned.1.call-update) | async-done | bytes 524304 | tf_op jit(solution)/shard_map/psum | solution.py:62
  463.7 1.1 copy.40
  464.8 1.0 fusion.19
  465.8 11.7 %cholesky.130 = f32[128,128]{1,0:T(8,128)S(1)} custom-call(f32[128,128]{1,0:T(8,128)S(1)} %cholesky.194), custom_call_target="Cholesky" | custom-call | tf_op jit(solution)/shard_map/jit(cholesky)/cholesky | solution.py:63
  477.6 9.8 %custom-call.13 = f32[1,128,128]{1,2,0:T(8,128)S(1)} custom-call(f32[1,128,128]{2,1,0:T(8,128)S(1)} %get-tuple-element.59), custom_call_target="InvertDiagBlocksLowerTriangular" | custom-call | tf_op jit(solution)/shard_map/jit(cholesky)/cholesky | solution.py:63
  487.9 11.7 %cholesky.147 = f32[128,128]{1,0:T(8,128)S(1)} custom-call(f32[128,128]{1,0:T(8,128)S(1)} %convolution_subtract_fusion.3), custom_call_target="Cholesky" | custom-call | tf_op jit(solution)/shard_map/jit(cholesky)/cholesky | solution.py:63
  501.7 4.0 while.4
  502.3 1.4 bitcast_dynamic-update-slice_fusion.4
  504.3 1.4 bitcast_dynamic-update-slice_fusion.4
  505.7 20.1 %custom-call.14 = f32[2,128,128]{1,2,0:T(8,128)S(1)} custom-call(f32[2,128,128]{2,1,0:T(8,128)S(1)} %get-tuple-element.18), custom_call_target="InvertDiagBlocksLowerTriangular" | custom-call | tf_op jit(solution)/shard_map/triangular_solve/custom-call.0 | solution.py:64
  526.4 1.0 convolution_subtract_fusion.1
  528.0 1.7 fusion.10
  529.8 0.8 copy.47
  530.7 75.4 %all-gather.9.cloned.1.call-done = f32[8192,256]{1,0:T(8,128)} async-done(((f32[256,256]{1,0:T(8,128)}), f32[8192,256]{1,0:T(8,128)}) %all-gather.9.cloned.1.call-update) | async-done | bytes 8388624 | tf_op jit(solution)/shard_map/all_gather | solution.py:70
  606.0 3.9 reduce_sum.19
  610.2 11.7 %cholesky.164 = f32[128,128]{1,0:T(8,128)S(1)} custom-call(f32[128,128]{1,0:T(8,128)S(1)} %cholesky.197), custom_call_target="Cholesky" | custom-call | tf_op jit(solution)/shard_map/jit(cholesky)/cholesky | solution.py:74
  621.9 9.8 %custom-call.15 = f32[1,128,128]{1,2,0:T(8,128)S(1)} custom-call(f32[1,128,128]{2,1,0:T(8,128)S(1)} %get-tuple-element.55), custom_call_target="InvertDiagBlocksLowerTriangular" | custom-call | tf_op jit(solution)/shard_map/jit(cholesky)/cholesky | solution.py:74
  632.2 11.9 %cholesky.181 = f32[128,128]{1,0:T(8,128)S(1)} custom-call(f32[128,128]{1,0:T(8,128)S(1)} %convolution_subtract_fusion.2), custom_call_target="Cholesky" | custom-call | tf_op jit(solution)/shard_map/jit(cholesky)/cholesky | solution.py:74
  646.9 4.1 while.5
  647.5 1.4 bitcast_dynamic-update-slice_fusion.5
  649.6 1.4 bitcast_dynamic-update-slice_fusion.5
  651.0 19.7 %custom-call.16 = f32[2,128,128]{1,2,0:T(8,128)S(1)} custom-call(f32[2,128,128]{2,1,0:T(8,128)S(1)} %get-tuple-element.19), custom_call_target="InvertDiagBlocksLowerTriangular" | custom-call | tf_op jit(solution)/shard_map/triangular_solve/custom-call.0 | solution.py:75
  672.7 1.0 copy.54
  (64 shorter events, 13.2 us)
Async XLA Ops:
  7.2 78.5 %all-gather.7.cloned.1.call-start = ((), (), s32[]{:S(2)}) async-start(), calls=%async_computation.4 | async-start | bytes 4718592 | tf_op jit(solution)/shard_map/all_gather | solution.py:32
  7.9 125.2 %all-gather.5.cloned.1.call-start = ((), (), s32[]{:S(2)}) async-start(), calls=%async_computation.2 | async-start | bytes 2621440 | tf_op jit(solution)/shard_map/all_gather | solution.py:31
  8.6 184.7 %reduce-scatter.5.cloned.1.call-start = ((), (), s32[]{:S(2)}) async-start(), calls=%async_computation.5 | async-start | bytes 5242880 | tf_op jit(solution)/shard_map/reduce_scatter | solution.py:59
  133.0 196.3 %reduce-scatter.3.cloned.1.call-start = ((), (), s32[]{:S(2)}) async-start(), calls=%async_computation.3 | async-start | bytes 9437184 | tf_op jit(solution)/shard_map/reduce_scatter | solution.py:50
  179.0 284.6 %all-reduce.6.cloned.1.call-start = ((), (), s32[]{:S(2)}) async-start(), calls=%async_computation.7 | async-start | bytes 1048576 | tf_op jit(solution)/shard_map/psum | solution.py:62
  184.6 3.4 copy-start
  188.8 1.8 copy-start.1
  333.5 272.5 %all-gather.9.cloned.1.call-start = ((), (), s32[]{:S(2)}) async-start(), calls=%async_computation.6 | async-start | bytes 8650752 | tf_op jit(solution)/shard_map/all_gather | solution.py:70
  465.8 64.0 %copy-start.2 = (f32[256,256]{0,1:T(8,128)S(1)}, f32[256,256]{0,1:T(8,128)}, u32[]{:S(2)}) copy-start(f32[256,256]{0,1:T(8,128)} %get-tuple-element.43) | copy-start | bytes 786436
Sparse Core Ops, SparseCore 0:
  10.1 75.5 all-gather.6
  87.2 21.0 all-gather.4
  133.1 45.1 reduce-scatter.4
  181.8 147.4 reduce-scatter.2
  335.2 128.4 all-reduce.5
  529.9 76.0 all-gather.8
